TPU v7x, 32 devices: a whole 2x2x4 slice. The times are simulated.
32 devices in a mesh: dp: 8 (over y, x, core), tensor: 4 (over z).
Axes of the slice: x: 2, y: 2, z: 4, core: 2. Of those that a mesh axis runs over, the one named last changes fastest.
Arguments:
- tokens: bfloat16 [8192, 2048], P(('dp', 'tensor')), may hold values from -6 to 6
- positions: int32 [8192], P('dp'), may hold values from 0 to 1023, as said below
- norm_gain: float32 [2, 2, 2048], replicated, may hold values from 0.25 to 1.75
- norm_bias: float32 [2, 2, 2048], replicated, may hold values from -3 to 3
- w_qkv: bfloat16 [2, 2048, 3, 2048], P(None, 'dp', None, 'tensor'), may hold values from -0.125 to 0.125
- b_qkv: float32 [2, 3, 2048], replicated, may hold values from -3 to 3
- w_out: bfloat16 [2, 2048, 2048], P(None, 'tensor', 'dp'), may hold values from -0.5 to 0.5
- w_gate_up: bfloat16 [2, 2048, 2, 5632], P(None, 'dp', None, 'tensor'), may hold values from -0.125 to 0.125
- w_down: bfloat16 [2, 5632, 2048], P(None, 'tensor', 'dp'), may hold values from -0.078125 to 0.078125
- cotangent: bfloat16 [8192, 2048], P(('dp', 'tensor')), may hold values from -6 to 6
Outputs:
- activations: bfloat16 [8192, 2048], P(('dp', 'tensor'))
- input_grad: float32 [8192, 2048], P(('dp', 'tensor'))
- gain_grad: float32 [2, 2, 2048], replicated
- norm_bias_grad: float32 [2, 2, 2048], replicated
- qkv_grad: float32 [2, 2048, 3, 2048], P(None, 'dp', None, 'tensor')
- qkv_bias_grad: float32 [2, 3, 2048], replicated
- out_grad: float32 [2, 2048, 2048], P(None, 'tensor', 'dp')
- gate_up_grad: float32 [2, 2048, 2, 5632], P(None, 'dp', None, 'tensor')
- down_grad: float32 [2, 5632, 2048], P(None, 'tensor', 'dp')
Inputs may be any that keep to these rules, and one draw needn't show every extreme that they name: positions[i] counts the tokens before i in its document; documents lie end to end in the sequences of 1024 tokens, so the first token of a sequence has 0 and every other token has 0 or one more than the token before it.
All inputs are finite; a program needn't handle non-finite values.
Results may differ from a plain program's by a relative error of at most 0.023.
Values may be sent and summed in bfloat16 or wider, within the bound.
A program may use at most 320 MiB of HBM per device.

v0:
```python
import math
import jax
import jax.numpy as jnp
from jax import lax
from jax.sharding import PartitionSpec as P

HD = 64
ROT = 16
LAYERS = 2
norm_eps = 1e-05
theta_log = math.log(10000.0)
masked_score = -1e30
contract_rows = (((0,), (0,)), ((), ()))
contract_cols = (((1,), (1,)), ((), ()))


def norm_parts(hidden):
    average = jnp.mean(hidden, axis=-1, keepdims=True)
    centred = hidden - average
    variance = jnp.mean(centred * centred, axis=-1, keepdims=True)
    inverse = lax.rsqrt(variance + norm_eps)
    return (centred * inverse, inverse)


def norm_back(grad_normed, scaled, inverse, norm_weight):
    weighted = grad_normed * norm_weight
    first_mean = jnp.mean(weighted, axis=-1, keepdims=True)
    second_mean = jnp.mean(weighted * scaled, axis=-1, keepdims=True)
    grad_input = inverse * (weighted - first_mean - scaled * second_mean)
    return (grad_input, jnp.sum(grad_normed * scaled, axis=0), jnp.sum(grad_normed, axis=0))


def rotary_tables(positions):
    half_rot = ROT // 2
    frequency = jnp.exp(-(jnp.arange(half_rot, dtype=jnp.float32) * 2.0 / ROT) * theta_log)
    angles = positions.astype(jnp.float32)[:, None] * frequency[None, :]
    return (jnp.cos(angles)[:, None, :], jnp.sin(angles)[:, None, :])


def rotate(values, cos_table, sin_table):
    half_rot = ROT // 2
    first_half = values[..., :half_rot]
    second_half = values[..., half_rot:ROT]
    return jnp.concatenate(
        [
            first_half * cos_table - second_half * sin_table,
            second_half * cos_table + first_half * sin_table,
            values[..., ROT:],
        ],
        axis=-1,
    )


def inner_rows(left, right):
    return lax.dot_general(left, right, contract_rows, preferred_element_type=jnp.float32)


def inner_cols(left, right):
    return lax.dot_general(left, right, contract_cols, preferred_element_type=jnp.float32)


def block_scores(queries, key_rows, positions, number, block_rows, score_scale):
    seq_len = key_rows.shape[0]
    row_start = number * block_rows
    query_block = lax.dynamic_slice_in_dim(queries, row_start, block_rows, 0)
    scores = (
        jnp.einsum("qhd,khd->hqk", query_block, key_rows, preferred_element_type=jnp.float32)
        * score_scale
    )
    row_index = row_start + jnp.arange(block_rows, dtype=jnp.int32)
    first_key = row_index - lax.dynamic_slice_in_dim(positions, row_start, block_rows, 0)
    columns = jnp.arange(seq_len, dtype=jnp.int32)
    allowed = (columns[None, :] <= row_index[:, None]) & (columns[None, :] >= first_key[:, None])
    return (query_block, allowed, jnp.where(allowed[None], scores, masked_score))


def attend_forward(queries, key_rows, values, positions, score_scale):
    seq_len = queries.shape[0]
    block_rows = min(512, seq_len)

    def one_block(number):
        query_block, allowed, scores = block_scores(
            queries, key_rows, positions, number, block_rows, score_scale
        )
        row_max = jnp.max(scores, axis=-1, keepdims=True)
        shifted = jnp.exp(scores - row_max)
        row_sum = jnp.sum(shifted, axis=-1, keepdims=True)
        weights_low = (shifted / row_sum).astype(jnp.bfloat16)
        block_out = jnp.einsum(
            "hqk,khd->qhd", weights_low, values, preferred_element_type=jnp.float32
        )
        return (block_out, row_max + jnp.log(row_sum))

    block_outs, logsums = lax.map(one_block, jnp.arange(seq_len // block_rows, dtype=jnp.int32))
    return (block_outs.reshape(seq_len, -1), logsums)


def attend_back(queries, key_rows, values, positions, logsums, grad_attended, score_scale):
    seq_len = queries.shape[0]
    block_rows = min(512, seq_len)

    def one_block(totals, inputs):
        grad_keys, grad_values = totals
        number, logsum = inputs
        query_block, allowed, scores = block_scores(
            queries, key_rows, positions, number, block_rows, score_scale
        )
        softmax_rows = jnp.exp(scores - logsum)
        grad_block = lax.dynamic_slice_in_dim(grad_attended, number * block_rows, block_rows, 0)
        grad_probs = jnp.einsum(
            "qhd,khd->hqk", grad_block, values, preferred_element_type=jnp.float32
        )
        grad_values = grad_values + jnp.einsum(
            "hqk,qhd->khd",
            softmax_rows.astype(jnp.bfloat16),
            grad_block,
            preferred_element_type=jnp.float32,
        )
        row_inner = jnp.sum(softmax_rows * grad_probs, axis=-1, keepdims=True)
        grad_scores = jnp.where(allowed[None], softmax_rows * (grad_probs - row_inner), 0.0).astype(
            jnp.bfloat16
        )
        grad_query = (
            jnp.einsum("hqk,khd->qhd", grad_scores, key_rows, preferred_element_type=jnp.float32)
            * score_scale
        )
        grad_keys = (
            grad_keys
            + jnp.einsum(
                "hqk,qhd->khd", grad_scores, query_block, preferred_element_type=jnp.float32
            )
            * score_scale
        )
        return ((grad_keys, grad_values), grad_query)

    empty_grad = jnp.zeros(key_rows.shape, jnp.float32)
    numbers = jnp.arange(seq_len // block_rows, dtype=jnp.int32)
    (grad_keys, grad_values), grad_queries = lax.scan(
        one_block, (empty_grad, empty_grad), (numbers, logsums)
    )
    return (grad_queries.reshape(queries.shape), grad_keys, grad_values)


def per_device(
    tokens, positions, norm_gain, norm_bias, w_qkv, b_qkv, w_out, w_gate_up, w_down, cotangent
):
    tensor_rank = lax.axis_index("tensor")
    width_local = w_qkv.shape[3]
    heads_local = width_local // HD
    ff_local = w_gate_up.shape[3]
    local_rows = tokens.shape[0]
    seq_len = positions.shape[0]
    score_scale = 1.0 / math.sqrt(HD)
    cos_table, sin_table = rotary_tables(positions)
    hidden = tokens.astype(jnp.float32)
    kept_state = []
    for layer_index in range(LAYERS):
        gathered = (
            lax.all_gather(w_qkv[layer_index], "dp", axis=0, tiled=True),
            lax.all_gather(w_out[layer_index], "dp", axis=1, tiled=True),
            lax.all_gather(w_gate_up[layer_index], "dp", axis=0, tiled=True),
            lax.all_gather(w_down[layer_index], "dp", axis=1, tiled=True),
        )
        full_qkv, full_out, full_gu, full_down = gathered
        scaled_a, inverse_a = norm_parts(hidden)
        normed_a = (scaled_a * norm_gain[layer_index, 0] + norm_bias[layer_index, 0]).astype(
            jnp.bfloat16
        )
        rows_a = lax.all_gather(normed_a, "tensor", axis=0, tiled=True)
        bias_local = lax.dynamic_slice_in_dim(
            b_qkv[layer_index], tensor_rank * width_local, width_local, 1
        )
        mixed = jnp.dot(
            rows_a,
            full_qkv.reshape(full_qkv.shape[0], 3 * width_local),
            preferred_element_type=jnp.float32,
        ) + bias_local.reshape(3 * width_local)
        mixed = mixed.reshape(seq_len, 3, heads_local, HD)
        queries = rotate(mixed[:, 0], cos_table, sin_table).astype(jnp.bfloat16)
        key_rows = rotate(mixed[:, 1], cos_table, sin_table).astype(jnp.bfloat16)
        values = mixed[:, 2].astype(jnp.bfloat16)
        attended, logsums = attend_forward(queries, key_rows, values, positions, score_scale)
        attended = attended.astype(jnp.bfloat16)

        def project_attn(row_start, row_count, source=attended, weight=full_out):
            return jnp.dot(source, weight, preferred_element_type=jnp.float32)

        branch_a = lax.psum_scatter(
            project_attn(jnp.int32(0), local_rows * lax.axis_size("tensor")).astype(jnp.bfloat16),
            "tensor",
            scatter_dimension=0,
            tiled=True,
        ).astype(jnp.float32)
        hidden_mid = hidden + branch_a
        scaled_b, inverse_b = norm_parts(hidden_mid)
        normed_b = (scaled_b * norm_gain[layer_index, 1] + norm_bias[layer_index, 1]).astype(
            jnp.bfloat16
        )
        rows_b = lax.all_gather(normed_b, "tensor", axis=0, tiled=True)
        gate_up = jnp.dot(
            rows_b,
            full_gu.reshape(full_gu.shape[0], 2 * ff_local),
            preferred_element_type=jnp.float32,
        ).reshape(seq_len, 2, ff_local)
        activated = (jax.nn.silu(gate_up[:, 0]) * gate_up[:, 1]).astype(jnp.bfloat16)

        def project_mlp(row_start, row_count, source=activated, weight=full_down):
            return jnp.dot(source, weight, preferred_element_type=jnp.float32)

        hidden = hidden_mid + lax.psum_scatter(
            project_mlp(jnp.int32(0), local_rows * lax.axis_size("tensor")).astype(jnp.bfloat16),
            "tensor",
            scatter_dimension=0,
            tiled=True,
        ).astype(jnp.float32)
        kept_state.append(
            (
                gathered,
                scaled_a,
                inverse_a,
                rows_a,
                queries,
                key_rows,
                values,
                logsums,
                attended,
                scaled_b,
                inverse_b,
                rows_b,
                gate_up,
                activated,
            )
        )
    activations = hidden.astype(jnp.bfloat16)
    grad = cotangent.astype(jnp.float32)
    weight_parts = [None] * LAYERS
    gain_rows = [None] * LAYERS
    shift_rows = [None] * LAYERS
    qkv_shift_rows = [None] * LAYERS
    for layer_index in reversed(range(LAYERS)):
        (
            gathered,
            scaled_a,
            inverse_a,
            rows_a,
            queries,
            key_rows,
            values,
            logsums,
            attended,
            scaled_b,
            inverse_b,
            rows_b,
            gate_up,
            activated,
        ) = kept_state[layer_index]
        full_qkv, full_out, full_gu, full_down = (
            lax.all_gather(w_qkv[layer_index], "dp", axis=0, tiled=True),
            lax.all_gather(w_out[layer_index], "dp", axis=1, tiled=True),
            lax.all_gather(w_gate_up[layer_index], "dp", axis=0, tiled=True),
            lax.all_gather(w_down[layer_index], "dp", axis=1, tiled=True),
        )
        grad_rows_b = lax.all_gather(grad.astype(jnp.bfloat16), "tensor", axis=0, tiled=True)
        grad_down_weight = inner_rows(activated, grad_rows_b)
        grad_act = inner_cols(grad_rows_b, full_down)
        gate_part = gate_up[:, 0]
        up_part = gate_up[:, 1]
        sigmoid_gate = jax.nn.sigmoid(gate_part)
        grad_gate = grad_act * up_part * sigmoid_gate * (1.0 + gate_part * (1.0 - sigmoid_gate))
        grad_up = grad_act * jax.nn.silu(gate_part)
        grad_gate_up = (
            jnp.stack([grad_gate, grad_up], axis=1)
            .astype(jnp.bfloat16)
            .reshape(seq_len, 2 * ff_local)
        )
        grad_gu_weight = inner_rows(rows_b, grad_gate_up).reshape(full_gu.shape)
        flat_gu = full_gu.reshape(full_gu.shape[0], 2 * ff_local)

        def back_mlp(row_start, row_count, source=grad_gate_up, weight=flat_gu):
            return inner_cols(source, weight)

        grad_normed_b = lax.psum_scatter(
            back_mlp(jnp.int32(0), local_rows * lax.axis_size("tensor")).astype(jnp.bfloat16),
            "tensor",
            scatter_dimension=0,
            tiled=True,
        ).astype(jnp.float32)
        grad_in_b, gain_b, shift_b = norm_back(
            grad_normed_b, scaled_b, inverse_b, norm_gain[layer_index, 1]
        )
        grad = grad + grad_in_b
        grad_rows_a = lax.all_gather(grad.astype(jnp.bfloat16), "tensor", axis=0, tiled=True)
        grad_out_weight = inner_rows(attended, grad_rows_a)
        grad_attended = inner_cols(grad_rows_a, full_out).astype(jnp.bfloat16)
        grad_attended = grad_attended.reshape(seq_len, heads_local, HD)
        grad_queries, grad_keys, grad_values = attend_back(
            queries, key_rows, values, positions, logsums, grad_attended, score_scale
        )
        grad_queries = rotate(grad_queries, cos_table, -sin_table)
        grad_keys = rotate(grad_keys, cos_table, -sin_table)
        grad_mixed = jnp.stack([grad_queries, grad_keys, grad_values], axis=1)
        grad_mixed = grad_mixed.reshape(seq_len, 3 * width_local).astype(jnp.bfloat16)
        qkv_shift_local = jnp.sum(grad_mixed, axis=0, dtype=jnp.float32).reshape(3, width_local)
        qkv_shift_rows[layer_index] = lax.dynamic_update_slice(
            jnp.zeros((3, b_qkv.shape[2]), jnp.float32),
            qkv_shift_local,
            (jnp.int32(0), tensor_rank * width_local),
        )
        grad_qkv_weight = inner_rows(rows_a, grad_mixed).reshape(full_qkv.shape)
        flat_qkv = full_qkv.reshape(full_qkv.shape[0], 3 * width_local)

        def back_attn(row_start, row_count, source=grad_mixed, weight=flat_qkv):
            return inner_cols(source, weight)

        grad_normed_a = lax.psum_scatter(
            back_attn(jnp.int32(0), local_rows * lax.axis_size("tensor")).astype(jnp.bfloat16),
            "tensor",
            scatter_dimension=0,
            tiled=True,
        ).astype(jnp.float32)
        grad_in_a, gain_a, shift_a = norm_back(
            grad_normed_a, scaled_a, inverse_a, norm_gain[layer_index, 0]
        )
        grad = grad + grad_in_a
        gain_rows[layer_index] = jnp.stack([gain_a, gain_b])
        shift_rows[layer_index] = jnp.stack([shift_a, shift_b])
        weight_parts[layer_index] = (
            lax.psum_scatter(
                grad_qkv_weight.astype(jnp.bfloat16), "dp", scatter_dimension=0, tiled=True
            ).astype(jnp.float32),
            lax.psum_scatter(
                grad_out_weight.astype(jnp.bfloat16), "dp", scatter_dimension=1, tiled=True
            ).astype(jnp.float32),
            lax.psum_scatter(
                grad_gu_weight.astype(jnp.bfloat16), "dp", scatter_dimension=0, tiled=True
            ).astype(jnp.float32),
            lax.psum_scatter(
                grad_down_weight.astype(jnp.bfloat16), "dp", scatter_dimension=1, tiled=True
            ).astype(jnp.float32),
        )
    stack_qkv = jnp.stack([weight_parts[number][0] for number in range(LAYERS)])
    stack_out = jnp.stack([weight_parts[number][1] for number in range(LAYERS)])
    stack_gu = jnp.stack([weight_parts[number][2] for number in range(LAYERS)])
    stack_down = jnp.stack([weight_parts[number][3] for number in range(LAYERS)])
    gain_grad, norm_bias_grad, qkv_bias_grad = lax.psum(
        (jnp.stack(gain_rows), jnp.stack(shift_rows), jnp.stack(qkv_shift_rows)), ("dp", "tensor")
    )
    return (
        activations,
        grad,
        gain_grad,
        norm_bias_grad,
        stack_qkv,
        qkv_bias_grad,
        stack_out,
        stack_gu,
        stack_down,
    )


def solution(mesh):
    in_specs = (
        P(("dp", "tensor"), None),
        P("dp"),
        P(),
        P(),
        P(None, "dp", None, "tensor"),
        P(),
        P(None, "tensor", "dp"),
        P(None, "dp", None, "tensor"),
        P(None, "tensor", "dp"),
        P(("dp", "tensor"), None),
    )
    out_specs = (
        P(("dp", "tensor"), None),
        P(("dp", "tensor"), None),
        P(),
        P(),
        P(None, "dp", None, "tensor"),
        P(),
        P(None, "tensor", "dp"),
        P(None, "dp", None, "tensor"),
        P(None, "tensor", "dp"),
    )
    return jax.shard_map(
        per_device, mesh=mesh, in_specs=in_specs, out_specs=out_specs, check_vma=False
    )
```

profile of v0, /device:TPU:1, one launch (start us, length us, event | category | flops | bytes accessed | tf_op | source)
XLA Modules:
  0.0 2722.3 jit_solution(6625782385930977792)
XLA Ops:
  20.9 78.1 %all-gather.25.cloned.1.call-done = bf16[1024,2048]{1,0:T(8,128)(2,1)} async-done(((bf16[256,2048]{1,0:T(8,128)(2,1)}), bf16[1024,2048]{1,0:T(8,128)(2,1)}) %all-gather.25.cloned.1.call-update) | async-done | bytes 4194320 | tf_op jit(solution)/shard_map/all_gather | solution.py:169
  99.0 48.1 %all-gather.41.cloned.1.call-done = bf16[1,2048,3,512]{1,3,2,0:T(8,128)(2,1)} async-done(((bf16[1,256,3,512]{1,3,2,0:T(8,128)(2,1)}), bf16[1,2048,3,512]{1,3,2,0:T(8,128)(2,1)}) %all-gather.41.cloned.1.call-update) | async-done | bytes 6291472 | tf_op jit(solution)/shard_map/all_gather | solution.py:159
  219.9 70.5 %reduce-scatter.17.cloned.1.call-done = bf16[256,2048]{1,0:T(8,128)(2,1)} async-done(((bf16[1024,2048]{1,0:T(8,128)(2,1)}), bf16[256,2048]{1,0:T(8,128)(2,1)}) %reduce-scatter.17.cloned.1.call-update) | async-done | bytes 1048592 | tf_op jit(solution)/shard_map/reduce_scatter | solution.py:188
  298.2 63.4 %all-gather.45.cloned.1.call-done = bf16[1,2048,2,1408]{3,1,2,0:T(8,128)(2,1)} async-done(((bf16[1,256,2,1408]{3,1,2,0:T(8,128)(2,1)}), bf16[1,2048,2,1408]{3,1,2,0:T(8,128)(2,1)}) %all-gather.45.cloned.1.call-update) | async-done | bytes 11534352 | tf_op jit(solution)/shard_map/all_gather | solution.py:161
  377.3 66.7 %all-gather.27.cloned.1.call-done = bf16[1024,2048]{1,0:T(8,128)(2,1)} async-done(((bf16[256,2048]{1,0:T(8,128)(2,1)}), bf16[1024,2048]{1,0:T(8,128)(2,1)}) %all-gather.27.cloned.1.call-update) | async-done | bytes 4194320 | tf_op jit(solution)/shard_map/all_gather | solution.py:199
  503.3 74.1 %reduce-scatter.19.cloned.1.call-done = bf16[256,2048]{1,0:T(8,128)(2,1)} async-done(((bf16[1024,2048]{1,0:T(8,128)(2,1)}), bf16[256,2048]{1,0:T(8,128)(2,1)}) %reduce-scatter.19.cloned.1.call-update) | async-done | bytes 1048592 | tf_op jit(solution)/shard_map/reduce_scatter | solution.py:210
  626.9 82.4 %all-gather.29.cloned.1.call-done = bf16[1024,2048]{1,0:T(8,128)(2,1)} async-done(((bf16[256,2048]{1,0:T(8,128)(2,1)}), bf16[1024,2048]{1,0:T(8,128)(2,1)}) %all-gather.29.cloned.1.call-update) | async-done | bytes 4194320 | tf_op jit(solution)/shard_map/all_gather | solution.py:169
  779.1 72.6 %reduce-scatter.21.cloned.1.call-done = bf16[256,2048]{1,0:T(8,128)(2,1)} async-done(((bf16[1024,2048]{1,0:T(8,128)(2,1)}), bf16[256,2048]{1,0:T(8,128)(2,1)}) %reduce-scatter.21.cloned.1.call-update) | async-done | bytes 1048592 | tf_op jit(solution)/shard_map/reduce_scatter | solution.py:188
  857.2 65.2 %all-gather.53.cloned.1.call-done = bf16[1,2048,2,1408]{3,1,2,0:T(8,128)(2,1)} async-done(((bf16[1,256,2,1408]{3,1,2,0:T(8,128)(2,1)}), bf16[1,2048,2,1408]{3,1,2,0:T(8,128)(2,1)}) %all-gather.53.cloned.1.call-update) | async-done | bytes 11534352 | tf_op jit(solution)/shard_map/all_gather | solution.py:161
  938.0 66.9 %all-gather.31.cloned.1.call-done = bf16[1024,2048]{1,0:T(8,128)(2,1)} async-done(((bf16[256,2048]{1,0:T(8,128)(2,1)}), bf16[1024,2048]{1,0:T(8,128)(2,1)}) %all-gather.31.cloned.1.call-update) | async-done | bytes 4194320 | tf_op jit(solution)/shard_map/all_gather | solution.py:199
  1023.7 62.0 %all-gather.33.cloned.1.call-done = bf16[1024,2048]{1,0:T(8,128)(2,1)} async-done(((bf16[256,2048]{1,0:T(8,128)(2,1)}), bf16[1024,2048]{1,0:T(8,128)(2,1)}) %all-gather.33.cloned.1.call-update) | async-done | bytes 4194320 | tf_op jit(solution)/shard_map/all_gather | solution.py:263
  1085.7 45.2 %all-gather.55.cloned.1.call-done = bf16[1,1408,2048]{2,1,0:T(8,128)(2,1)} async-done(((bf16[1,1408,256]{2,1,0:T(8,128)(2,1)}), bf16[1,1408,2048]{2,1,0:T(8,128)(2,1)}) %all-gather.55.cloned.1.call-update) | async-done | bytes 5767184 | tf_op jit(solution)/shard_map/all_gather | solution.py:162
  1182.0 58.3 %reduce-scatter.25.cloned.1.call-done = bf16[256,2048]{1,0:T(8,128)(2,1)} async-done(((bf16[1024,2048]{1,0:T(8,128)(2,1)}), bf16[256,2048]{1,0:T(8,128)(2,1)}) %reduce-scatter.25.cloned.1.call-update) | async-done | bytes 1048592 | tf_op jit(solution)/shard_map/reduce_scatter | solution.py:282
  1243.1 76.6 %reduce-scatter.23.cloned.1.call-done = bf16[256,2048]{1,0:T(8,128)(2,1)} async-done(((bf16[1024,2048]{1,0:T(8,128)(2,1)}), bf16[256,2048]{1,0:T(8,128)(2,1)}) %reduce-scatter.23.cloned.1.call-update) | async-done | bytes 1048592 | tf_op jit(solution)/shard_map/reduce_scatter | solution.py:210
  1324.5 81.3 %all-gather.35.cloned.1.call-done = bf16[1024,2048]{1,0:T(8,128)(2,1)} async-done(((bf16[256,2048]{1,0:T(8,128)(2,1)}), bf16[1024,2048]{1,0:T(8,128)(2,1)}) %all-gather.35.cloned.1.call-update) | async-done | bytes 4194320 | tf_op jit(solution)/shard_map/all_gather | solution.py:292
  1414.1 183.7 %while.56 = (s32[]{:T(128)}, f32[1024,8,64]{0,2,1:T(8,128)}, f32[1024,8,64]{0,2,1:T(8,128)S(1)}, f32[2,512,8,64]{1,0,3,2:T(2,128)}, s32[2]{0:T(128)S(1)}, /*inde...) while((s32[]{:T(128)}, f32[1024,8,64]{0,2,1:T(8,128)}, ...), condition=%wide.region_25.26_spmd.clone, body=%wide.region_23.25_spmd.clone.sunk | while | flops 2747542528 | bytes 239134992 | solution.py:138
  1618.3 75.4 %reduce-scatter.27.cloned.1.call-done = bf16[256,2048]{1,0:T(8,128)(2,1)} async-done(((bf16[1024,2048]{1,0:T(8,128)(2,1)}), bf16[256,2048]{1,0:T(8,128)(2,1)}) %reduce-scatter.27.cloned.1.call-update) | async-done | bytes 1048592 | tf_op jit(solution)/shard_map/reduce_scatter | solution.py:315
  1699.3 81.4 %all-gather.37.cloned.1.call-done = bf16[1024,2048]{1,0:T(8,128)(2,1)} async-done(((bf16[256,2048]{1,0:T(8,128)(2,1)}), bf16[1024,2048]{1,0:T(8,128)(2,1)}) %all-gather.37.cloned.1.call-update) | async-done | bytes 4194320 | tf_op jit(solution)/shard_map/all_gather | solution.py:263
  1814.0 75.4 %reduce-scatter.29.cloned.1.call-done = bf16[256,2048]{1,0:T(8,128)(2,1)} async-done(((bf16[1024,2048]{1,0:T(8,128)(2,1)}), bf16[256,2048]{1,0:T(8,128)(2,1)}) %reduce-scatter.29.cloned.1.call-update) | async-done | bytes 1048592 | tf_op jit(solution)/shard_map/reduce_scatter | solution.py:282
  2010.9 198.1 %while.57 = (s32[]{:T(128)}, f32[1024,8,64]{0,2,1:T(8,128)}, f32[1024,8,64]{0,2,1:T(8,128)}, f32[2,512,8,64]{1,0,3,2:T(2,128)}, s32[2]{0:T(128)S(1)}, /*index=5*...) while((s32[]{:T(128)}, f32[1024,8,64]{0,2,1:T(8,128)}, ...), condition=%wide.region_34.35_spmd.clone, body=%wide.region_32.34_spmd.clone.sunk | while | flops 2747542528 | bytes 239134992 | solution.py:138
  2373.2 77.0 %reduce-scatter.31.cloned.1.call-done = bf16[256,2048]{1,0:T(8,128)(2,1)} async-done(((bf16[1024,2048]{1,0:T(8,128)(2,1)}), bf16[256,2048]{1,0:T(8,128)(2,1)}) %reduce-scatter.31.cloned.1.call-update) | async-done | bytes 1048592 | tf_op jit(solution)/shard_map/reduce_scatter | solution.py:315
  2457.2 58.6 %reduce-scatter.35.cloned.1.call-done = bf16[256,3,512]{2,0,1:T(8,128)(2,1)} async-done(((bf16[2048,3,512]{2,0,1:T(8,128)(2,1)}), bf16[256,3,512]{2,0,1:T(8,128)(2,1)}) %reduce-scatter.35.cloned.1.call-update) | async-done | bytes 786448 | tf_op jit(solution)/shard_map/reduce_scatter | solution.py:328
  2515.8 65.6 %reduce-scatter.33.cloned.1.call-done = bf16[256,3,512]{2,0,1:T(8,128)(2,1)} async-done(((bf16[2048,3,512]{2,0,1:T(8,128)(2,1)}), bf16[256,3,512]{2,0,1:T(8,128)(2,1)}) %reduce-scatter.33.cloned.1.call-update) | async-done | bytes 786448 | tf_op jit(solution)/shard_map/reduce_scatter | solution.py:328
  2584.6 126.3 %all-reduce.3.cloned.1.call-done = (f32[2,2,2048]{2,1,0:T(2,128)}, f32[2,2,2048]{2,1,0:T(2,128)}, f32[2,3,2048]{2,0,1:T(2,128)}) async-done(((f32[2,2,2048]{2,1,0:T(2,128)}, f32[2,2,2048]{2,1,0:T(2,128)}, f32[2,3,2048]{2,0,1:T(2,128)}), (f32[2,2,2048]{2,1,0:T(2,128)}, f32[2,2,2048]{2,1,0:T(2,128)}, f32[2,3,2048]{2,0,1:T(2,128)})) %all-reduce.3.cloned.1.call-update) | async-done | bytes 114704 | tf_op jit(solution)/shard_map/psum | solution.py:345
  (507 shorter events, 1193.7 us)
Async XLA Ops:
  18.4 189.1 %all-gather.43.cloned.1.call-start = ((), (), s32[]{:S(2)}) async-start(), calls=%async_computation.41 | async-start | bytes 2359296 | tf_op jit(solution)/shard_map/all_gather | solution.py:160
  19.3 271.1 %reduce-scatter.17.cloned.1.call-start = ((), (), s32[]{:S(2)}) async-start(), calls=%async_computation.17 | async-start | bytes 5242880 | tf_op jit(solution)/shard_map/reduce_scatter | solution.py:188
  219.9 224.1 %all-gather.27.cloned.1.call-start = ((), (), s32[]{:S(2)}) async-start(), calls=%async_computation.18 | async-start | bytes 5242880 | tf_op jit(solution)/shard_map/all_gather | solution.py:199
  296.8 193.1 %all-gather.47.cloned.1.call-start = ((), (), s32[]{:S(2)}) async-start(), calls=%async_computation.43 | async-start | bytes 6488064 | tf_op jit(solution)/shard_map/all_gather | solution.py:162
  298.1 279.3 %reduce-scatter.19.cloned.1.call-start = ((), (), s32[]{:S(2)}) async-start(), calls=%async_computation.19 | async-start | bytes 5242880 | tf_op jit(solution)/shard_map/reduce_scatter | solution.py:210
  503.2 206.0 %all-gather.29.cloned.1.call-start = ((), (), s32[]{:S(2)}) async-start(), calls=%async_computation.20 | async-start | bytes 5242880 | tf_op jit(solution)/shard_map/all_gather | solution.py:169
  582.6 269.1 %reduce-scatter.21.cloned.1.call-start = ((), (), s32[]{:S(2)}) async-start(), calls=%async_computation.21 | async-start | bytes 5242880 | tf_op jit(solution)/shard_map/reduce_scatter | solution.py:188
  779.1 225.8 %all-gather.31.cloned.1.call-start = ((), (), s32[]{:S(2)}) async-start(), calls=%async_computation.22 | async-start | bytes 5242880 | tf_op jit(solution)/shard_map/all_gather | solution.py:199
  856.0 229.7 %all-gather.33.cloned.1.call-start = ((), (), s32[]{:S(2)}) async-start(), calls=%async_computation.24 | async-start | bytes 5242880 | tf_op jit(solution)/shard_map/all_gather | solution.py:263
  856.6 274.3 %all-gather.55.cloned.1.call-start = ((), (), s32[]{:S(2)}) async-start(), calls=%async_computation.47 | async-start | bytes 6488064 | tf_op jit(solution)/shard_map/all_gather | solution.py:162
  857.1 383.2 %reduce-scatter.25.cloned.1.call-start = ((), (), s32[]{:S(2)}) async-start(), calls=%async_computation.25 | async-start | bytes 5242880 | tf_op jit(solution)/shard_map/reduce_scatter | solution.py:282
  1181.9 223.9 %all-gather.35.cloned.1.call-start = ((), (), s32[]{:S(2)}) async-start(), calls=%async_computation.26 | async-start | bytes 5242880 | tf_op jit(solution)/shard_map/all_gather | solution.py:292
  1324.5 369.3 %reduce-scatter.27.cloned.1.call-start = ((), (), s32[]{:S(2)}) async-start(), calls=%async_computation.27 | async-start | bytes 5242880 | tf_op jit(solution)/shard_map/reduce_scatter | solution.py:315
  1699.3 190.2 %reduce-scatter.29.cloned.1.call-start = ((), (), s32[]{:S(2)}) async-start(), calls=%async_computation.29 | async-start | bytes 5242880 | tf_op jit(solution)/shard_map/reduce_scatter | solution.py:282
  1895.4 359.9 %reduce-scatter.47.cloned.1.call-start = ((), (), s32[]{:S(2)}) async-start(), calls=%async_computation.39 | async-start | bytes 6488064 | tf_op jit(solution)/shard_map/reduce_scatter | solution.py:337
  1906.1 349.2 %reduce-scatter.45.cloned.1.call-start = ((), (), s32[]{:S(2)}) async-start(), calls=%async_computation.38 | async-start | bytes 6488064 | tf_op jit(solution)/shard_map/reduce_scatter | solution.py:337
  1918.7 340.5 %reduce-scatter.43.cloned.1.call-start = ((), (), s32[]{:S(2)}) async-start(), calls=%async_computation.37 | async-start | bytes 12976128 | tf_op jit(solution)/shard_map/reduce_scatter | solution.py:334
  1953.1 328.6 %reduce-scatter.41.cloned.1.call-start = ((), (), s32[]{:S(2)}) async-start(), calls=%async_computation.36 | async-start | bytes 12976128 | tf_op jit(solution)/shard_map/reduce_scatter | solution.py:334
  1987.7 338.8 %reduce-scatter.39.cloned.1.call-start = ((), (), s32[]{:S(2)}) async-start(), calls=%async_computation.35 | async-start | bytes 2359296 | tf_op jit(solution)/shard_map/reduce_scatter | solution.py:331
  1995.5 375.6 %reduce-scatter.37.cloned.1.call-start = ((), (), s32[]{:S(2)}) async-start(), calls=%async_computation.34 | async-start | bytes 2359296 | tf_op jit(solution)/shard_map/reduce_scatter | solution.py:331
  2001.5 448.7 %reduce-scatter.31.cloned.1.call-start = ((), (), s32[]{:S(2)}) async-start(), calls=%async_computation.31 | async-start | bytes 5242880 | tf_op jit(solution)/shard_map/reduce_scatter | solution.py:315
  2228.3 287.6 %reduce-scatter.35.cloned.1.call-start = ((), (), s32[]{:S(2)}) async-start(), calls=%async_computation.33 | async-start | bytes 7077888 | tf_op jit(solution)/shard_map/reduce_scatter | solution.py:328
  2241.3 340.1 %reduce-scatter.33.cloned.1.call-start = ((), (), s32[]{:S(2)}) async-start(), calls=%async_computation.32 | async-start | bytes 7077888 | tf_op jit(solution)/shard_map/reduce_scatter | solution.py:328
  2254.4 456.5 %all-reduce.3.cloned.1.call-start = ((), (), s32[]{:S(2)}) async-start(), calls=%async_computation.48 | async-start | bytes 229376 | tf_op jit(solution)/shard_map/psum | solution.py:345
  (109 other events, 4705.9 us)
Sparse Core Ops, SparseCore 0:
  16.1 82.8 all-gather.24
  214.1 76.3 reduce-scatter.16
  292.9 68.5 all-gather.44
  363.6 80.3 all-gather.26
  501.0 76.3 reduce-scatter.18
  628.8 80.3 all-gather.28
  776.5 75.1 reduce-scatter.20
  853.8 68.5 all-gather.52
  924.5 80.3 all-gather.30
  1006.3 79.2 all-gather.32
  1163.9 76.3 reduce-scatter.24
  1242.5 77.2 reduce-scatter.22
  1324.6 81.2 all-gather.34
  1618.4 75.2 reduce-scatter.26
  1699.4 81.2 all-gather.36
  1814.1 75.2 reduce-scatter.28
  1895.5 81.2 all-gather.38
  2041.5 59.0 reduce-scatter.44
  2104.3 86.8 reduce-scatter.42
  2194.9 86.7 reduce-scatter.40
  2373.3 76.8 reduce-scatter.30
  2453.6 62.1 reduce-scatter.34
  2519.6 61.7 reduce-scatter.32
  2587.8 123.0 all-reduce.2
  (9 shorter events, 374.5 us)
where the time goes:
time: 2740 us; the launch traced here: 2720 us
  waiting for transfers between devices  1740 us (64%)
  matrix products  597 us (22%)
  local copies, waits for them, and re-layouts  255 us (9%)
  other arithmetic  105 us (4%)
    all_gather x4, waiting for transfers between devices, per_device(): lax.all_gather(grad.astype(jnp.bfloat16), 'tensor', axis=0, tiled=True)  225 us
    all_gather x2, waiting for transfers between devices, per_device(): rows_a = lax.all_gather(normed_a, 'tensor', axis=0, tiled=True)  160 us
    reduce_scatter x2, waiting for transfers between devices, per_device(): lax.psum_scatter(back_attn(jnp.int32(0), local_rows * lax.axis_size('tens...  152 us
    reduce_scatter x2, waiting for transfers between devices, per_device(): lax.psum_scatter(project_mlp(jnp.int32(0), local_rows * lax.axis_size('te...  151 us
    reduce_scatter x2, waiting for transfers between devices, per_device(): lax.psum_scatter(project_attn(jnp.int32(0), local_rows * lax.axis_size('t...  143 us
    reduce_scatter x2, waiting for transfers between devices, per_device(): lax.psum_scatter(back_mlp(jnp.int32(0), local_rows * lax.axis_size('tenso...  134 us
    all_gather x2, waiting for transfers between devices, per_device(): rows_b = lax.all_gather(normed_b, 'tensor', axis=0, tiled=True)  134 us
    all_gather x2, waiting for transfers between devices, per_device(): lax.all_gather(w_gate_up[layer_index], 'dp', axis=0, tiled=True)  129 us
  transfers between devices with their start and end apart: 33, of which 27 were waited for; matrix products, arithmetic and copies ran while one was open for 22% of the time, Pallas kernels for 0%

commit v1 on v0

--- a/solution.py
+++ b/solution.py
@@ -166,7 +166,33 @@
         normed_a = (scaled_a * norm_gain[layer_index, 0] + norm_bias[layer_index, 0]).astype(
             jnp.bfloat16
         )
-        rows_a = lax.all_gather(normed_a, "tensor", axis=0, tiled=True)
+        fields = []
+        carry, back, block_last = (
+            lax.axis_size("tensor"),
+            lax.axis_index("tensor"),
+            normed_a.shape[0],
+        )
+        for dev_i in range(carry):
+            fields.append((dev_i, (dev_i + 1) % carry))
+        ledger = []
+        for dev_i in range(carry):
+            ledger.append((dev_i, (dev_i - 1) % carry))
+        rows_a = jnp.zeros(
+            (*normed_a.shape[:0], carry * block_last, *normed_a.shape[0 + 1 :]), normed_a.dtype
+        )
+        w1 = k_now = normed_a
+        f_next = carry // 2
+        rows_a = lax.dynamic_update_slice_in_dim(rows_a, normed_a, back * block_last, axis=0)
+        for c in range(1, f_next + 1):
+            w1 = lax.ppermute(w1, "tensor", fields)
+            rows_a = lax.dynamic_update_slice_in_dim(
+                rows_a, w1, (back - c) % carry * block_last, axis=0
+            )
+            if c < carry - f_next:
+                k_now = lax.ppermute(k_now, "tensor", perm=ledger)
+                rows_a = lax.dynamic_update_slice_in_dim(
+                    rows_a, k_now, (back + c) % carry * block_last, axis=0
+                )
         bias_local = lax.dynamic_slice_in_dim(
             b_qkv[layer_index], tensor_rank * width_local, width_local, 1
         )

time: 2740 us -> 2640 us (0.964)
  waiting for transfers between devices: 1740 us -> 1600 us
    all_gather x2 -> x0, waiting for transfers between devices: 160 us -> none  [per_device(): rows_a = lax.all_gather(normed_a, 'tensor', axis=0, tiled=True)]
    ppermute x0 -> x6, waiting for transfers between devices: none -> 112 us  [the longest x4 77.8 us: per_device(): w1 = lax.ppermute(w1, 'tensor', fields)]
    all_gather x2, waiting for transfers between devices: 91.6 us -> 0.01 us  [per_device(): lax.all_gather(w_qkv[layer_index], 'dp', axis=0, tiled=True)]
  transfers between devices with their start and end apart: 33 -> 37, of which waited for: 27 -> 29; matrix products, arithmetic and copies ran while one was open for 22% -> 24% of each run, Pallas kernels for 0% -> 0%
where the time goes in v1:
time: 2640 us; the launch traced here: 2620 us
  waiting for transfers between devices  1600 us (61%)
  matrix products  597 us (23%)
  local copies, waits for them, and re-layouts  278 us (11%)
  other arithmetic  101 us (4%)
    all_gather x4, waiting for transfers between devices, per_device(): lax.all_gather(grad.astype(jnp.bfloat16), 'tensor', axis=0, tiled=True)  225 us
    reduce_scatter x2, waiting for transfers between devices, per_device(): lax.psum_scatter(back_attn(jnp.int32(0), local_rows * lax.axis_size('tens...  153 us
    reduce_scatter x2, waiting for transfers between devices, per_device(): lax.psum_scatter(project_mlp(jnp.int32(0), local_rows * lax.axis_size('te...  151 us
    reduce_scatter x2, waiting for transfers between devices, per_device(): lax.psum_scatter(project_attn(jnp.int32(0), local_rows * lax.axis_size('t...  147 us
    all_gather x2, waiting for transfers between devices, per_device(): rows_b = lax.all_gather(normed_b, 'tensor', axis=0, tiled=True)  134 us
    reduce_scatter x2, waiting for transfers between devices, per_device(): lax.psum_scatter(back_mlp(jnp.int32(0), local_rows * lax.axis_size('tenso...  134 us
    all_gather x2, waiting for transfers between devices, per_device(): lax.all_gather(w_gate_up[layer_index], 'dp', axis=0, tiled=True)  129 us
    psum x1, waiting for transfers between devices, per_device(): lax.psum((jnp.stack(gain_rows), jnp.stack(shift_rows), jnp.stack(qkv_shif...  126 us
  transfers between devices with their start and end apart: 37, of which 29 were waited for; matrix products, arithmetic and copies ran while one was open for 24% of the time, Pallas kernels for 0%

profile of v1, /device:TPU:1, one launch (start us, length us, event | category | flops | bytes accessed | tf_op | source)
XLA Modules:
  0.0 2624.1 jit_solution(6986607758530658549)
XLA Ops:
  111.2 42.5 %while.54 = (s32[]{:T(128)}, bf16[2,512,8,64]{1,3,2,0:T(8,128)(2,1)}, f32[2,8,512,1]{2,1,3,0:T(8,128)S(1)}, s32[2]{0:T(128)S(1)}, s32[1024]{0:T(1024)S(1)}, /*in...) while((s32[]{:T(128)}, ...), condition=%wide.region_5.6_spmd, body=%wide.region_2.5_spmd.sunk | while | flops 1125643264 | bytes 64628996 | solution.py:94
  170.5 72.4 %reduce-scatter.17.cloned.1.call-done = bf16[256,2048]{1,0:T(8,128)(2,1)} async-done(((bf16[1024,2048]{1,0:T(8,128)(2,1)}), bf16[256,2048]{1,0:T(8,128)(2,1)}) %reduce-scatter.17.cloned.1.call-update) | async-done | bytes 1048592 | tf_op jit(solution)/shard_map/reduce_scatter | solution.py:214
  250.4 63.6 %all-gather.39.cloned.1.call-done = bf16[1,2048,2,1408]{3,1,2,0:T(8,128)(2,1)} async-done(((bf16[1,256,2,1408]{3,1,2,0:T(8,128)(2,1)}), bf16[1,2048,2,1408]{3,1,2,0:T(8,128)(2,1)}) %all-gather.39.cloned.1.call-update) | async-done | bytes 11534352 | tf_op jit(solution)/shard_map/all_gather | solution.py:161
  329.4 67.1 %all-gather.23.cloned.1.call-done = bf16[1024,2048]{1,0:T(8,128)(2,1)} async-done(((bf16[256,2048]{1,0:T(8,128)(2,1)}), bf16[1024,2048]{1,0:T(8,128)(2,1)}) %all-gather.23.cloned.1.call-update) | async-done | bytes 4194320 | tf_op jit(solution)/shard_map/all_gather | solution.py:225
  455.5 74.2 %reduce-scatter.19.cloned.1.call-done = bf16[256,2048]{1,0:T(8,128)(2,1)} async-done(((bf16[1024,2048]{1,0:T(8,128)(2,1)}), bf16[256,2048]{1,0:T(8,128)(2,1)}) %reduce-scatter.19.cloned.1.call-update) | async-done | bytes 1048592 | tf_op jit(solution)/shard_map/reduce_scatter | solution.py:236
  676.9 74.2 %reduce-scatter.21.cloned.1.call-done = bf16[256,2048]{1,0:T(8,128)(2,1)} async-done(((bf16[1024,2048]{1,0:T(8,128)(2,1)}), bf16[256,2048]{1,0:T(8,128)(2,1)}) %reduce-scatter.21.cloned.1.call-update) | async-done | bytes 1048592 | tf_op jit(solution)/shard_map/reduce_scatter | solution.py:214
  756.8 65.0 %all-gather.47.cloned.1.call-done = bf16[1,2048,2,1408]{3,1,2,0:T(8,128)(2,1)} async-done(((bf16[1,256,2,1408]{3,1,2,0:T(8,128)(2,1)}), bf16[1,2048,2,1408]{3,1,2,0:T(8,128)(2,1)}) %all-gather.47.cloned.1.call-update) | async-done | bytes 11534352 | tf_op jit(solution)/shard_map/all_gather | solution.py:161
  837.4 66.9 %all-gather.25.cloned.1.call-done = bf16[1024,2048]{1,0:T(8,128)(2,1)} async-done(((bf16[256,2048]{1,0:T(8,128)(2,1)}), bf16[1024,2048]{1,0:T(8,128)(2,1)}) %all-gather.25.cloned.1.call-update) | async-done | bytes 4194320 | tf_op jit(solution)/shard_map/all_gather | solution.py:225
  923.1 62.1 %all-gather.27.cloned.1.call-done = bf16[1024,2048]{1,0:T(8,128)(2,1)} async-done(((bf16[256,2048]{1,0:T(8,128)(2,1)}), bf16[1024,2048]{1,0:T(8,128)(2,1)}) %all-gather.27.cloned.1.call-update) | async-done | bytes 4194320 | tf_op jit(solution)/shard_map/all_gather | solution.py:289
  985.3 45.2 %all-gather.49.cloned.1.call-done = bf16[1,1408,2048]{2,1,0:T(8,128)(2,1)} async-done(((bf16[1,1408,256]{2,1,0:T(8,128)(2,1)}), bf16[1,1408,2048]{2,1,0:T(8,128)(2,1)}) %all-gather.49.cloned.1.call-update) | async-done | bytes 5767184 | tf_op jit(solution)/shard_map/all_gather | solution.py:162
  1081.4 58.5 %reduce-scatter.25.cloned.1.call-done = bf16[256,2048]{1,0:T(8,128)(2,1)} async-done(((bf16[1024,2048]{1,0:T(8,128)(2,1)}), bf16[256,2048]{1,0:T(8,128)(2,1)}) %reduce-scatter.25.cloned.1.call-update) | async-done | bytes 1048592 | tf_op jit(solution)/shard_map/reduce_scatter | solution.py:308
  1142.8 76.6 %reduce-scatter.23.cloned.1.call-done = bf16[256,2048]{1,0:T(8,128)(2,1)} async-done(((bf16[1024,2048]{1,0:T(8,128)(2,1)}), bf16[256,2048]{1,0:T(8,128)(2,1)}) %reduce-scatter.23.cloned.1.call-update) | async-done | bytes 1048592 | tf_op jit(solution)/shard_map/reduce_scatter | solution.py:236
  1224.2 81.3 %all-gather.29.cloned.1.call-done = bf16[1024,2048]{1,0:T(8,128)(2,1)} async-done(((bf16[256,2048]{1,0:T(8,128)(2,1)}), bf16[1024,2048]{1,0:T(8,128)(2,1)}) %all-gather.29.cloned.1.call-update) | async-done | bytes 4194320 | tf_op jit(solution)/shard_map/all_gather | solution.py:318
  1313.7 183.9 %while.56 = (s32[]{:T(128)}, f32[1024,8,64]{0,2,1:T(8,128)}, f32[1024,8,64]{0,2,1:T(8,128)S(1)}, f32[2,512,8,64]{1,0,3,2:T(2,128)}, s32[2]{0:T(128)S(1)}, /*inde...) while((s32[]{:T(128)}, f32[1024,8,64]{0,2,1:T(8,128)}, ...), condition=%wide.region_25.26_spmd.clone, body=%wide.region_23.25_spmd.clone.sunk | while | flops 2747542528 | bytes 239134992 | solution.py:138
  1518.1 75.4 %reduce-scatter.27.cloned.1.call-done = bf16[256,2048]{1,0:T(8,128)(2,1)} async-done(((bf16[1024,2048]{1,0:T(8,128)(2,1)}), bf16[256,2048]{1,0:T(8,128)(2,1)}) %reduce-scatter.27.cloned.1.call-update) | async-done | bytes 1048592 | tf_op jit(solution)/shard_map/reduce_scatter | solution.py:341
  1600.3 81.4 %all-gather.31.cloned.1.call-done = bf16[1024,2048]{1,0:T(8,128)(2,1)} async-done(((bf16[256,2048]{1,0:T(8,128)(2,1)}), bf16[1024,2048]{1,0:T(8,128)(2,1)}) %all-gather.31.cloned.1.call-update) | async-done | bytes 4194320 | tf_op jit(solution)/shard_map/all_gather | solution.py:289
  1714.7 75.4 %reduce-scatter.29.cloned.1.call-done = bf16[256,2048]{1,0:T(8,128)(2,1)} async-done(((bf16[1024,2048]{1,0:T(8,128)(2,1)}), bf16[256,2048]{1,0:T(8,128)(2,1)}) %reduce-scatter.29.cloned.1.call-update) | async-done | bytes 1048592 | tf_op jit(solution)/shard_map/reduce_scatter | solution.py:308
  1913.0 198.2 %while.57 = (s32[]{:T(128)}, f32[1024,8,64]{0,2,1:T(8,128)}, f32[1024,8,64]{0,2,1:T(8,128)}, f32[2,512,8,64]{1,0,3,2:T(2,128)}, s32[2]{0:T(128)S(1)}, /*index=5*...) while((s32[]{:T(128)}, f32[1024,8,64]{0,2,1:T(8,128)}, ...), condition=%wide.region_34.35_spmd.clone, body=%wide.region_32.34_spmd.clone.sunk | while | flops 2747542528 | bytes 239134992 | solution.py:138
  2193.1 35.5 %reduce-scatter.39.cloned.1.call-done = bf16[512,256]{1,0:T(8,128)(2,1)} async-done(((bf16[512,2048]{1,0:T(8,128)(2,1)}), bf16[512,256]{1,0:T(8,128)(2,1)}) %reduce-scatter.39.cloned.1.call-update) | async-done | bytes 262160 | tf_op jit(solution)/shard_map/reduce_scatter | solution.py:357
  2228.6 44.4 %reduce-scatter.37.cloned.1.call-done = bf16[512,256]{1,0:T(8,128)(2,1)} async-done(((bf16[512,2048]{1,0:T(8,128)(2,1)}), bf16[512,256]{1,0:T(8,128)(2,1)}) %reduce-scatter.37.cloned.1.call-update) | async-done | bytes 262160 | tf_op jit(solution)/shard_map/reduce_scatter | solution.py:357
  2275.0 77.1 %reduce-scatter.31.cloned.1.call-done = bf16[256,2048]{1,0:T(8,128)(2,1)} async-done(((bf16[1024,2048]{1,0:T(8,128)(2,1)}), bf16[256,2048]{1,0:T(8,128)(2,1)}) %reduce-scatter.31.cloned.1.call-update) | async-done | bytes 1048592 | tf_op jit(solution)/shard_map/reduce_scatter | solution.py:341
  2359.2 58.6 %reduce-scatter.35.cloned.1.call-done = bf16[256,3,512]{2,0,1:T(8,128)(2,1)} async-done(((bf16[2048,3,512]{2,0,1:T(8,128)(2,1)}), bf16[256,3,512]{2,0,1:T(8,128)(2,1)}) %reduce-scatter.35.cloned.1.call-update) | async-done | bytes 786448 | tf_op jit(solution)/shard_map/reduce_scatter | solution.py:354
  2417.8 65.4 %reduce-scatter.33.cloned.1.call-done = bf16[256,3,512]{2,0,1:T(8,128)(2,1)} async-done(((bf16[2048,3,512]{2,0,1:T(8,128)(2,1)}), bf16[256,3,512]{2,0,1:T(8,128)(2,1)}) %reduce-scatter.33.cloned.1.call-update) | async-done | bytes 786448 | tf_op jit(solution)/shard_map/reduce_scatter | solution.py:354
  2486.5 126.5 %all-reduce.3.cloned.1.call-done = (f32[2,2,2048]{2,1,0:T(2,128)}, f32[2,2,2048]{2,1,0:T(2,128)}, f32[2,3,2048]{2,0,1:T(2,128)}) async-done(((f32[2,2,2048]{2,1,0:T(2,128)}, f32[2,2,2048]{2,1,0:T(2,128)}, f32[2,3,2048]{2,0,1:T(2,128)}), (f32[2,2,2048]{2,1,0:T(2,128)}, f32[2,2,2048]{2,1,0:T(2,128)}, f32[2,3,2048]{2,0,1:T(2,128)})) %all-reduce.3.cloned.1.call-update) | async-done | bytes 114704 | tf_op jit(solution)/shard_map/psum | solution.py:371
  (527 shorter events, 1177.1 us)
Async XLA Ops:
  19.6 223.3 %reduce-scatter.17.cloned.1.call-start = ((), (), s32[]{:S(2)}) async-start(), calls=%async_computation.16 | async-start | bytes 5242880 | tf_op jit(solution)/shard_map/reduce_scatter | solution.py:214
  170.5 226.0 %all-gather.23.cloned.1.call-start = ((), (), s32[]{:S(2)}) async-start(), calls=%async_computation.17 | async-start | bytes 5242880 | tf_op jit(solution)/shard_map/all_gather | solution.py:225
  249.1 193.1 %all-gather.41.cloned.1.call-start = ((), (), s32[]{:S(2)}) async-start(), calls=%async_computation.41 | async-start | bytes 6488064 | tf_op jit(solution)/shard_map/all_gather | solution.py:162
  250.4 279.3 %reduce-scatter.19.cloned.1.call-start = ((), (), s32[]{:S(2)}) async-start(), calls=%async_computation.18 | async-start | bytes 5242880 | tf_op jit(solution)/shard_map/reduce_scatter | solution.py:236
  455.4 212.4 %all-gather.45.cloned.1.call-start = ((), (), s32[]{:S(2)}) async-start(), calls=%async_computation.43 | async-start | bytes 2359296 | tf_op jit(solution)/shard_map/all_gather | solution.py:160
  559.2 192.0 %reduce-scatter.21.cloned.1.call-start = ((), (), s32[]{:S(2)}) async-start(), calls=%async_computation.19 | async-start | bytes 5242880 | tf_op jit(solution)/shard_map/reduce_scatter | solution.py:214
  676.9 227.4 %all-gather.25.cloned.1.call-start = ((), (), s32[]{:S(2)}) async-start(), calls=%async_computation.20 | async-start | bytes 5242880 | tf_op jit(solution)/shard_map/all_gather | solution.py:225
  755.4 229.8 %all-gather.27.cloned.1.call-start = ((), (), s32[]{:S(2)}) async-start(), calls=%async_computation.22 | async-start | bytes 5242880 | tf_op jit(solution)/shard_map/all_gather | solution.py:289
  756.2 274.3 %all-gather.49.cloned.1.call-start = ((), (), s32[]{:S(2)}) async-start(), calls=%async_computation.45 | async-start | bytes 6488064 | tf_op jit(solution)/shard_map/all_gather | solution.py:162
  756.8 383.2 %reduce-scatter.25.cloned.1.call-start = ((), (), s32[]{:S(2)}) async-start(), calls=%async_computation.23 | async-start | bytes 5242880 | tf_op jit(solution)/shard_map/reduce_scatter | solution.py:308
  1081.4 224.1 %all-gather.29.cloned.1.call-start = ((), (), s32[]{:S(2)}) async-start(), calls=%async_computation.24 | async-start | bytes 5242880 | tf_op jit(solution)/shard_map/all_gather | solution.py:318
  1224.1 369.4 %reduce-scatter.27.cloned.1.call-start = ((), (), s32[]{:S(2)}) async-start(), calls=%async_computation.25 | async-start | bytes 5242880 | tf_op jit(solution)/shard_map/reduce_scatter | solution.py:341
  1600.2 189.9 %reduce-scatter.29.cloned.1.call-start = ((), (), s32[]{:S(2)}) async-start(), calls=%async_computation.27 | async-start | bytes 5242880 | tf_op jit(solution)/shard_map/reduce_scatter | solution.py:308
  1714.7 182.9 %all-gather.33.cloned.1.call-start = ((), (), s32[]{:S(2)}) async-start(), calls=%async_computation.28 | async-start | bytes 5242880 | tf_op jit(solution)/shard_map/all_gather | solution.py:318
  1797.3 360.3 %reduce-scatter.47.cloned.1.call-start = ((), (), s32[]{:S(2)}) async-start(), calls=%async_computation.37 | async-start | bytes 6488064 | tf_op jit(solution)/shard_map/reduce_scatter | solution.py:363
  1808.1 349.5 %reduce-scatter.45.cloned.1.call-start = ((), (), s32[]{:S(2)}) async-start(), calls=%async_computation.36 | async-start | bytes 6488064 | tf_op jit(solution)/shard_map/reduce_scatter | solution.py:363
  1820.7 340.8 %reduce-scatter.43.cloned.1.call-start = ((), (), s32[]{:S(2)}) async-start(), calls=%async_computation.35 | async-start | bytes 12976128 | tf_op jit(solution)/shard_map/reduce_scatter | solution.py:360
  1855.3 328.5 %reduce-scatter.41.cloned.1.call-start = ((), (), s32[]{:S(2)}) async-start(), calls=%async_computation.34 | async-start | bytes 12976128 | tf_op jit(solution)/shard_map/reduce_scatter | solution.py:360
  1889.7 338.9 %reduce-scatter.39.cloned.1.call-start = ((), (), s32[]{:S(2)}) async-start(), calls=%async_computation.33 | async-start | bytes 2359296 | tf_op jit(solution)/shard_map/reduce_scatter | solution.py:357
  1897.6 375.4 %reduce-scatter.37.cloned.1.call-start = ((), (), s32[]{:S(2)}) async-start(), calls=%async_computation.32 | async-start | bytes 2359296 | tf_op jit(solution)/shard_map/reduce_scatter | solution.py:357
  1903.6 448.6 %reduce-scatter.31.cloned.1.call-start = ((), (), s32[]{:S(2)}) async-start(), calls=%async_computation.29 | async-start | bytes 5242880 | tf_op jit(solution)/shard_map/reduce_scatter | solution.py:341
  2130.7 287.1 %reduce-scatter.35.cloned.1.call-start = ((), (), s32[]{:S(2)}) async-start(), calls=%async_computation.31 | async-start | bytes 7077888 | tf_op jit(solution)/shard_map/reduce_scatter | solution.py:354
  2143.7 339.5 %reduce-scatter.33.cloned.1.call-start = ((), (), s32[]{:S(2)}) async-start(), calls=%async_computation.30 | async-start | bytes 7077888 | tf_op jit(solution)/shard_map/reduce_scatter | solution.py:354
  2156.7 456.3 %all-reduce.3.cloned.1.call-start = ((), (), s32[]{:S(2)}) async-start(), calls=%async_computation.46 | async-start | bytes 229376 | tf_op jit(solution)/shard_map/psum | solution.py:371
  (111 other events, 4422.9 us)
Sparse Core Ops, SparseCore 0:
  11.1 49.1 all-gather.34
  164.5 78.3 reduce-scatter.16
  245.4 68.5 all-gather.38
  316.1 80.3 all-gather.22
  453.3 76.3 reduce-scatter.18
  674.3 76.7 reduce-scatter.20
  753.2 68.5 all-gather.46
  823.9 80.3 all-gather.24
  906.0 79.2 all-gather.26
  1063.5 76.3 reduce-scatter.24
  1142.1 77.2 reduce-scatter.22
  1224.2 81.2 all-gather.28
  1518.2 75.2 reduce-scatter.26
  1600.4 81.2 all-gather.30
  1714.8 75.2 reduce-scatter.28
  1797.4 81.2 all-gather.32
  1882.5 57.5 reduce-scatter.46
  1943.6 58.9 reduce-scatter.44
  2006.4 86.7 reduce-scatter.42
  2097.1 86.7 reduce-scatter.40
  2275.4 76.7 reduce-scatter.30
  2355.6 62.2 reduce-scatter.34
  2421.4 61.7 reduce-scatter.32
  2489.8 123.0 all-reduce.2
  (7 shorter events, 273.4 us)
